TPU v7x, 128 devices: a whole 4x4x4 slice. The times are simulated.
128 devices in a mesh: sector: 32 (over z, y, x_hi), axial: 2 (over core), radial: 2 (over x_lo).
Axes of the slice: x: 4 (x_hi: 2, x_lo: 2; x = x_hi * 2 + x_lo), y: 4, z: 4, core: 2. Of those that a mesh axis runs over, the one named last changes fastest.
Arguments:
- state: float32 [64, 5, 16, 4096], P('axial', None, 'radial', 'sector'), may hold values from -6 to 6
- block_inverse: float32 [64, 5, 5, 16, 4096], P('axial', None, None, 'radial', 'sector'), may hold values from -2.1 to 2.1
- lower_rate: float32 [64, 16, 4096], P('axial', 'radial', 'sector'), may hold values from 0.5 to 2
- upper_rate: float32 [64, 16, 4096], P('axial', 'radial', 'sector'), may hold values from 0.5 to 2
- lower_jac: float32 [5, 5], replicated, may hold values from -1 to 1, as said below
- upper_jac: float32 [5, 5], replicated, may hold values from -1 to 1, as said below
- parcel_state: float32 [6, 2, 2, 1048576], P(None, 'axial', 'radial', 'sector'), may hold values from -4 to 4, as said below
- parcel_cell: int32 [2, 2, 1048576], P('axial', 'radial', 'sector'), may hold values from 0 to 32639
- parcel_count: int32 [2, 2, 32], P('axial', 'radial', 'sector'), may hold values from 4096 to 32768, as said below
Outputs:
- state_next: float32 [64, 5, 16, 4096], P('axial', None, 'radial', 'sector')
- parcel_left: float32 [2, 2, 1048576], P('axial', 'radial', 'sector')
Inputs may be any that keep to these rules, and one draw needn't show every extreme that they name: `parcel_count`: some block has all 32768 slots live. `lower_jac`: symmetric. `upper_jac`: symmetric. `parcel_state`: fields 0 and 1 are positive.
All inputs are finite; a program needn't handle non-finite values.
Results may differ from a plain program's by a relative error of at most 0.00021.
Values sent between devices are 32-bit elements; how exact they have to be, the bound alone decides.
A program may use at most 128 MiB of HBM per device.

v0:
```python
import functools

import jax
import jax.numpy as jnp
from jax import lax
from jax.experimental import pallas as pl
from jax.experimental.pallas import tpu as pltpu
from jax.sharding import PartitionSpec as P

F32 = jnp.float32
BF = jnp.bfloat16
MESH = pl.DeviceIdType.MESH
NT = (((1,), (1,)), ((), ()))
DIFFUSE = 0.15
SWIRL = 0.6
CH = 16


def sum5(terms):
    return ((terms[0] + terms[1]) + (terms[2] + terms[3])) + terms[4]


def rows16(row, times):
    packed = jnp.broadcast_to(row, (16, 128)).astype(BF)
    return jnp.concatenate([packed] * times, axis=0)


def one_hots(cells, oh, mk):
    row = lax.shift_right_logical(cells, 7).astype(F32)
    lane = (cells & 127).astype(F32)
    index = lax.broadcasted_iota(jnp.int32, (256, 128), 0).astype(F32).astype(BF)
    one, zero = jnp.ones((), BF), jnp.zeros((), BF)
    for j in range(CH):
        at = slice(j * 128, (j + 1) * 128)
        oh[:, at] = jnp.where(index == rows16(row[j : j + 1], 16), one, zero)
        mk[:, at] = jnp.where(index[:128] == rows16(lane[j : j + 1], 8), one, zero)


def kernel(
    nsec,
    state, binv, lrate, urate, ljac, ujac, parcels, cell, count,
    out, left,
    sx, bv, lv, uv, cv, pbuf, gas, g2, oh, mk, w, acc, res, tgt, edge,
    rsend, rrecv, upsend, uprecv, dnsend, dnrecv, face, fsend,
    lsem, psend, precv, hsend, hrecv, rlsend, rlrecv,
):
    s, a, r = lax.axis_index("sector"), lax.axis_index("axial"), lax.axis_index("radial")
    nxt, prv = lax.rem(s + 1, nsec), lax.rem(s + nsec - 1, nsec)
    steps = 256 // CH

    local = [
        pltpu.make_async_copy(state, sx.at[pl.ds(5, 160)], lsem.at[0]),
        pltpu.make_async_copy(cell, cv, lsem.at[1]),
        pltpu.make_async_copy(binv, bv, lsem.at[2]),
        pltpu.make_async_copy(lrate, lv, lsem.at[3]),
        pltpu.make_async_copy(urate, uv, lsem.at[4]),
    ]
    for copy in local:
        copy.start()

    barrier = pltpu.get_barrier_semaphore()
    for device in ((nxt, a, r), (prv, a, r), (s, 1 - a, r), (s, a, 1 - r)):
        pl.semaphore_signal(barrier, inc=1, device_id=device, device_id_type=MESH)
    pl.semaphore_wait(barrier, 4)

    def remote(src, dst, ssem, rsem, device):
        return pltpu.make_async_remote_copy(
            src_ref=src, dst_ref=dst, send_sem=ssem, recv_sem=rsem, device_id=device, device_id_type=MESH
        )

    def parcel_copy(c):
        rows = pl.ds(pl.multiple_of(c * CH, CH), CH)
        return remote(parcels.at[:, rows], pbuf.at[:, rows], psend.at[c], precv.at[c], (nxt, a, r))

    local[0].wait()

    def pack_radial(k, carry):
        rows = [
            jnp.where(r == 0, sx[5 + k * 5 + u, 7:8, :], sx[5 + k * 5 + u, 0:1, :]) for u in range(5)
        ]
        rsend[k] = jnp.concatenate(rows + [jnp.zeros((3, 128), F32)], axis=0)
        return carry

    lax.fori_loop(0, 32, pack_radial, 0)
    for q in range(10):
        turned = sx[5 + 16 * q : 21 + 16 * q].reshape(128, 128).T
        upsend[q : q + 1] = turned[127:128]
        dnsend[q : q + 1] = turned[0:1]
    halo = [
        remote(state.at[pl.ds(155 * (1 - a), 5)], sx.at[pl.ds(165 * a, 5)], hsend.at[0], hrecv.at[0], (s, 1 - a, r)),
        remote(rsend, rrecv, hsend.at[1], hrecv.at[1], (s, a, 1 - r)),
        remote(upsend, uprecv, hsend.at[2], hrecv.at[2], (nxt, a, r)),
        remote(dnsend, dnrecv, hsend.at[3], hrecv.at[3], (prv, a, r)),
    ]
    for copy in halo:
        copy.start()

    def send_parcels(c, carry):
        parcel_copy(c).start()
        return carry

    lax.fori_loop(0, steps, send_parcels, 0)

    for h in range(2):
        tile = jnp.concatenate([sx[5 + (16 * h + k) * 5 + 4] for k in range(16)], axis=0)
        turned = tile.T
        hi = turned.astype(BF)
        g2[0:128, h * 128 : (h + 1) * 128] = hi
        g2[128:256, h * 128 : (h + 1) * 128] = (turned - hi.astype(F32)).astype(BF)
    local[1].wait()

    def gather(i, carry):
        rows = pl.ds(pl.multiple_of(i * CH, CH), CH)
        one_hots(cv[rows], oh, mk)
        found = jnp.dot(g2[...], oh[...], preferred_element_type=F32)
        picked = (found[:128] + found[128:]) * mk[...].astype(F32)
        total = jnp.sum(jnp.sum(picked.reshape(16, 8, CH * 128), axis=0), axis=0, keepdims=True)
        for j in range(CH):
            gas[pl.ds(i * CH + j, 1), :] = total[:, j * 128 : (j + 1) * 128]
        return carry

    lax.fori_loop(0, steps, gather, 0)

    @pl.when(a == 0)
    def _():
        sx[0:5] = jnp.zeros((5, 8, 128), F32)

    @pl.when(a == 1)
    def _():
        sx[165:170] = jnp.zeros((5, 8, 128), F32)

    for copy in halo:
        copy.wait_recv()
    sub = lax.broadcasted_iota(jnp.int32, (128, 128), 0)
    for q in range(10):
        both = jnp.where(
            sub == 0,
            (DIFFUSE + SWIRL) * uprecv[q : q + 1],
            jnp.where(sub == 127, DIFFUSE * dnrecv[q : q + 1], 0.0),
        )
        edge[16 * q : 16 * q + 16] = both.T.reshape(16, 8, 128)
    sub8 = lax.broadcasted_iota(jnp.int32, (8, 128), 0)
    lane8 = lax.broadcasted_iota(jnp.int32, (8, 128), 1)
    seam = sub8 == 7 * (1 - r)

    def flux(k, carry):
        ring = rrecv[k]
        for u in range(5):
            i = k * 5 + u
            x = sx[5 + i]
            radial = (
                jnp.where(sub8 == 0, 0.0, pltpu.roll(x, 1, 0))
                + jnp.where(sub8 == 7, 0.0, pltpu.roll(x, 7, 0))
                + jnp.where(seam, jnp.broadcast_to(ring[u : u + 1], (8, 128)), 0.0)
            )
            below = jnp.where(lane8 == 0, 0.0, pltpu.roll(x, 1, 1))
            above = jnp.where(lane8 == 127, 0.0, pltpu.roll(x, 127, 1))
            beside = (sx[i] + sx[i + 10]) + (radial + above)
            res[i] = (
                DIFFUSE * beside + (DIFFUSE + SWIRL) * below + edge[i] - (6.0 * DIFFUSE + SWIRL) * x
            )
        return carry

    lax.fori_loop(0, 32, flux, 0)

    acc[...] = jnp.zeros_like(acc)
    live_count = count[0]

    def scatter(i, carry):
        parcel_copy(i).wait_recv()
        rows = pl.ds(pl.multiple_of(i * CH, CH), CH)
        one_hots(cv[rows], oh, mk)
        fields = [pbuf[f, rows] for f in range(6)]
        slot = (lax.broadcasted_iota(jnp.int32, (CH, 128), 0) + i * CH) * 128 + lax.broadcasted_iota(
            jnp.int32, (CH, 128), 1
        )
        mass = jnp.where(slot < live_count, fields[0], 0.0)
        frac = 1.0 - jnp.exp(-fields[1] * (1.0 + 0.5 * jnp.tanh(gas[rows])))
        evap = mass * frac
        left[rows] = mass * (1.0 - frac)
        deposits = [evap] + [evap * fields[f] for f in range(2, 6)]
        for v in range(5):
            hi = deposits[v].astype(BF).astype(F32)
            for half, piece in enumerate((hi, deposits[v] - hi)):
                for j in range(CH):
                    at = (half * CH + j) * 128
                    w[v * 128 : (v + 1) * 128, at : at + 128] = mk[:, j * 128 : (j + 1) * 128] * rows16(
                        piece[j : j + 1], 8
                    )
        width = CH * 128
        acc[...] += lax.dot_general(w[:, :width], oh[...], NT, preferred_element_type=F32) + lax.dot_general(
            w[:, width:], oh[...], NT, preferred_element_type=F32
        )
        return carry

    lax.fori_loop(0, steps, scatter, 0)
    for v in range(5):
        turned = acc[v * 128 : (v + 1) * 128].T
        for k in range(32):
            res[k * 5 + v] += turned[8 * k : 8 * k + 8]

    for copy in local[2:]:
        copy.wait()
    zeros = tuple(jnp.zeros((8, 128), F32) for _ in range(5))

    def product(jac, values):
        return [sum5([jac[u, v] * values[v] for v in range(5)]) for u in range(5)]

    def plane(k, carry, rate, jac, first, final):
        pushed = product(jac, carry)
        base = k * 5
        rk = rate[k]
        net = []
        for u in range(5):
            term = rk * pushed[u]
            r_u = res[base + u]
            if first:
                d = r_u - term
                tgt[base + u] = d
            else:
                d = tgt[base + u] - term
                if not final:
                    tgt[base + u] = r_u - term
            net.append(d)
        value = tuple(sum5([bv[k * 25 + u * 5 + v] * net[v] for v in range(5)]) for u in range(5))
        if final:
            for u in range(5):
                out[base + u] = sx[5 + base + u] + value[u]
        return value

    def relay(h):
        return remote(fsend.at[h], face.at[h], rlsend.at[h], rlrecv.at[h], (s, 1 - a, r))

    def half_sweep(hop, forward, first, final):
        sender = 0 if forward else 1

        @pl.when(a == 1 - sender)
        def _():
            relay(hop).wait_recv()

        @pl.when(a == sender)
        def _():
            face[hop] = jnp.zeros((5, 8, 128), F32)

        inflow = tuple(face[hop, u] for u in range(5))
        rate, jac = (lv, ljac) if forward else (uv, ujac)

        def body(i, carry):
            k = i if forward else 31 - i
            return plane(k, carry, rate, jac, first, final)

        last = lax.fori_loop(0, 32, body, inflow)

        @pl.when(a == sender)
        def _():
            for u in range(5):
                fsend[hop, u] = last[u]
            relay(hop).start()

    half_sweep(0, True, True, False)
    half_sweep(1, False, False, False)
    half_sweep(2, True, False, False)
    half_sweep(3, False, False, True)

    for hop in range(4):
        @pl.when(a == hop % 2)
        def _():
            relay(hop).wait_send()

    for copy in halo:
        copy.wait_send()

    def sent(c, carry):
        parcel_copy(c).wait_send()
        return carry

    lax.fori_loop(0, steps, sent, 0)


def solution(mesh):
    nsec = mesh.shape["sector"]

    def local(state, block_inverse, lower_rate, upper_rate, lower_jac, upper_jac, parcel_state, parcel_cell, parcel_count):
        hbm = pl.BlockSpec(memory_space=pl.ANY)
        vmem = pl.BlockSpec(memory_space=pltpu.VMEM)
        smem = pl.BlockSpec(memory_space=pltpu.SMEM)
        width = CH * 128
        dma = pltpu.SemaphoreType.DMA
        steps = 256 // CH
        out, left = pl.pallas_call(
            functools.partial(kernel, nsec),
            out_shape=(
                jax.ShapeDtypeStruct((160, 8, 128), F32),
                jax.ShapeDtypeStruct((256, 128), F32),
            ),
            in_specs=[hbm, hbm, hbm, hbm, smem, smem, hbm, hbm, smem],
            out_specs=(vmem, vmem),
            scratch_shapes=[
                pltpu.VMEM((170, 8, 128), F32),
                pltpu.VMEM((800, 8, 128), F32),
                pltpu.VMEM((32, 8, 128), F32),
                pltpu.VMEM((32, 8, 128), F32),
                pltpu.VMEM((256, 128), jnp.int32),
                pltpu.VMEM((6, 256, 128), F32),
                pltpu.VMEM((256, 128), F32),
                pltpu.VMEM((256, 256), BF),
                pltpu.VMEM((256, width), BF),
                pltpu.VMEM((128, width), BF),
                pltpu.VMEM((640, 2 * width), BF),
                pltpu.VMEM((640, 256), F32),
                pltpu.VMEM((160, 8, 128), F32),
                pltpu.VMEM((160, 8, 128), F32),
                pltpu.VMEM((160, 8, 128), F32),
                pltpu.VMEM((32, 8, 128), F32),
                pltpu.VMEM((32, 8, 128), F32),
                pltpu.VMEM((16, 128), F32),
                pltpu.VMEM((16, 128), F32),
                pltpu.VMEM((16, 128), F32),
                pltpu.VMEM((16, 128), F32),
                pltpu.VMEM((4, 5, 8, 128), F32),
                pltpu.VMEM((4, 5, 8, 128), F32),
                dma((5,)),
                dma((steps,)),
                dma((steps,)),
                dma((4,)),
                dma((4,)),
                dma((4,)),
                dma((4,)),
            ],
            compiler_params=pltpu.CompilerParams(
                collective_id=0, has_side_effects=True, vmem_limit_bytes=56 << 20
            ),
        )(
            state.reshape(160, 8, 128),
            block_inverse.reshape(800, 8, 128),
            lower_rate,
            upper_rate,
            lower_jac,
            upper_jac,
            parcel_state.reshape(6, 256, 128),
            parcel_cell.reshape(256, 128),
            parcel_count.reshape(1),
        )
        return out.reshape(state.shape), left.reshape(parcel_cell.shape)

    return jax.shard_map(
        local,
        mesh=mesh,
        in_specs=(
            P("axial", None, "radial", "sector"),
            P("axial", None, None, "radial", "sector"),
            P("axial", "radial", "sector"),
            P("axial", "radial", "sector"),
            P(),
            P(),
            P(None, "axial", "radial", "sector"),
            P("axial", "radial", "sector"),
            P("axial", "radial", "sector"),
        ),
        out_specs=(P("axial", None, "radial", "sector"), P("axial", "radial", "sector")),
        check_vma=False,
    )
```

profile of v0, /device:TPU:1, one launch (start us, length us, event | category | flops | bytes accessed | tf_op | source)
XLA Modules:
  0.0 69.2 jit_solution(9403334265864682711)
XLA Ops:
  1.3 64.3 %shard_map.104 = (f32[160,8,128]{2,1,0:T(8,128)}, f32[256,128]{1,0:T(8,128)}) custom-call(f32[160,8,128]{2,1,0:T(8,128)} %bitcast.11, f32[800,8,128]{2,1,0:T(8,128)} %bitcast.8, f32[32,8,128]{2,1,0:T(8,128)} %lrate.1, f32[32,8,128]{2,1,0:T(8,128)} %urate.1, f32[5,5]{1,0:T(8,128)} %ljac.1, f32[5,5]{1,0:T(8,128)} %ujac.1, f32[6,256,128]{2,1,0:T(8,128)} %bitcast.9, ...), custom_call_target="tpu_custom_call" | custom-call | tf_op jit(solution)/shard_map/pallas_call | solution.py:290
  65.6 2.0 %copy.14 = f32[32,5,8,128]{3,2,1,0:T(8,128)} copy(f32[32,5,8,128]{3,2,1,0:T(8,128)} %bitcast.10) | data formatting | bytes 1310720
  67.6 1.6 %copy.15 = f32[1,1,32768]{2,1,0:T(1,128)} copy(f32[1,1,32768]{2,1,0:T(1,128)} %bitcast.12) | data formatting | bytes 262144
where the time goes:
time: 69.4 us; the launch traced here: 69.2 us
  Pallas kernels  64.3 us (93%)
  local copies, waits for them, and re-layouts  3.53 us (5%)
  between operations  1.29 us (2%)
    pallas_call x1, Pallas kernels, local(): pl.pallas_call(functools.partial(kernel, nsec), out_shape=(jax.ShapeDtype...  64.3 us
    unnamed x2, local copies, waits for them, and re-layouts  3.53 us

commit v1 on v0

--- a/solution.py
+++ b/solution.py
@@ -9,11 +9,13 @@
 
 F32 = jnp.float32
 BF = jnp.bfloat16
+F8 = jnp.float8_e4m3fn
 MESH = pl.DeviceIdType.MESH
 NT = (((1,), (1,)), ((), ()))
 DIFFUSE = 0.15
 SWIRL = 0.6
-CH = 16
+CH = 32
+LOW = 8192.0
 
 
 def sum5(terms):
@@ -25,22 +27,24 @@
     return jnp.concatenate([packed] * times, axis=0)
 
 
-def one_hots(cells, oh, mk):
+def one_hots(cells, i, oh, oh8, mk):
     row = lax.shift_right_logical(cells, 7).astype(F32)
     lane = (cells & 127).astype(F32)
     index = lax.broadcasted_iota(jnp.int32, (256, 128), 0).astype(F32).astype(BF)
     one, zero = jnp.ones((), BF), jnp.zeros((), BF)
     for j in range(CH):
         at = slice(j * 128, (j + 1) * 128)
-        oh[:, at] = jnp.where(index == rows16(row[j : j + 1], 16), one, zero)
-        mk[:, at] = jnp.where(index[:128] == rows16(lane[j : j + 1], 8), one, zero)
+        hot = jnp.where(index == rows16(row[j : j + 1], 16), one, zero)
+        oh[i, :, at] = hot
+        oh8[i, :, at] = hot.astype(F8)
+        mk[i, :, at] = jnp.where(index[:128] == rows16(lane[j : j + 1], 8), one, zero)
 
 
 def kernel(
     nsec,
     state, binv, lrate, urate, ljac, ujac, parcels, cell, count,
     out, left,
-    sx, bv, lv, uv, cv, pbuf, gas, g2, oh, mk, w, acc, res, tgt, edge,
+    sx, bv, lv, uv, cv, pbuf, gas, g2, oh, oh8, mk, w, w8, acc, res, tgt, edge,
     rsend, rrecv, upsend, uprecv, dnsend, dnrecv, face, fsend,
     lsem, psend, precv, hsend, hrecv, rlsend, rlrecv,
 ):
@@ -61,7 +65,6 @@
     barrier = pltpu.get_barrier_semaphore()
     for device in ((nxt, a, r), (prv, a, r), (s, 1 - a, r), (s, a, 1 - r)):
         pl.semaphore_signal(barrier, inc=1, device_id=device, device_id_type=MESH)
-    pl.semaphore_wait(barrier, 4)
 
     def remote(src, dst, ssem, rsem, device):
         return pltpu.make_async_remote_copy(
@@ -74,18 +77,19 @@
 
     local[0].wait()
 
-    def pack_radial(k, carry):
-        rows = [
-            jnp.where(r == 0, sx[5 + k * 5 + u, 7:8, :], sx[5 + k * 5 + u, 0:1, :]) for u in range(5)
-        ]
-        rsend[k] = jnp.concatenate(rows + [jnp.zeros((3, 128), F32)], axis=0)
-        return carry
-
-    lax.fori_loop(0, 32, pack_radial, 0)
+    for i in range(160):
+        rsend[i : i + 1] = jnp.where(r == 0, sx[5 + i, 7:8, :], sx[5 + i, 0:1, :])
     for q in range(10):
         turned = sx[5 + 16 * q : 21 + 16 * q].reshape(128, 128).T
         upsend[q : q + 1] = turned[127:128]
         dnsend[q : q + 1] = turned[0:1]
+    for h in range(2):
+        tile = jnp.concatenate([sx[5 + (16 * h + k) * 5 + 4] for k in range(16)], axis=0)
+        turned = tile.T
+        hi = turned.astype(BF)
+        g2[0:128, h * 128 : (h + 1) * 128] = hi
+        g2[128:256, h * 128 : (h + 1) * 128] = (turned - hi.astype(F32)).astype(BF)
+    pl.semaphore_wait(barrier, 4)
     halo = [
         remote(state.at[pl.ds(155 * (1 - a), 5)], sx.at[pl.ds(165 * a, 5)], hsend.at[0], hrecv.at[0], (s, 1 - a, r)),
         remote(rsend, rrecv, hsend.at[1], hrecv.at[1], (s, a, 1 - r)),
@@ -101,19 +105,13 @@
 
     lax.fori_loop(0, steps, send_parcels, 0)
 
-    for h in range(2):
-        tile = jnp.concatenate([sx[5 + (16 * h + k) * 5 + 4] for k in range(16)], axis=0)
-        turned = tile.T
-        hi = turned.astype(BF)
-        g2[0:128, h * 128 : (h + 1) * 128] = hi
-        g2[128:256, h * 128 : (h + 1) * 128] = (turned - hi.astype(F32)).astype(BF)
     local[1].wait()
 
     def gather(i, carry):
         rows = pl.ds(pl.multiple_of(i * CH, CH), CH)
-        one_hots(cv[rows], oh, mk)
-        found = jnp.dot(g2[...], oh[...], preferred_element_type=F32)
-        picked = (found[:128] + found[128:]) * mk[...].astype(F32)
+        one_hots(cv[rows], i, oh, oh8, mk)
+        found = jnp.dot(g2[...], oh[i], preferred_element_type=F32)
+        picked = (found[:128] + found[128:]) * mk[i].astype(F32)
         total = jnp.sum(jnp.sum(picked.reshape(16, 8, CH * 128), axis=0), axis=0, keepdims=True)
         for j in range(CH):
             gas[pl.ds(i * CH + j, 1), :] = total[:, j * 128 : (j + 1) * 128]
@@ -144,14 +142,13 @@
     seam = sub8 == 7 * (1 - r)
 
     def flux(k, carry):
-        ring = rrecv[k]
         for u in range(5):
             i = k * 5 + u
             x = sx[5 + i]
             radial = (
                 jnp.where(sub8 == 0, 0.0, pltpu.roll(x, 1, 0))
                 + jnp.where(sub8 == 7, 0.0, pltpu.roll(x, 7, 0))
-                + jnp.where(seam, jnp.broadcast_to(ring[u : u + 1], (8, 128)), 0.0)
+                + jnp.where(seam, jnp.broadcast_to(rrecv[pl.ds(i, 1)], (8, 128)), 0.0)
             )
             below = jnp.where(lane8 == 0, 0.0, pltpu.roll(x, 1, 1))
             above = jnp.where(lane8 == 127, 0.0, pltpu.roll(x, 127, 1))
@@ -161,7 +158,7 @@
             )
         return carry
 
-    lax.fori_loop(0, 32, flux, 0)
+    lax.fori_loop(0, 32, flux, 0, unroll=4)
 
     acc[...] = jnp.zeros_like(acc)
     live_count = count[0]
@@ -169,7 +166,6 @@
     def scatter(i, carry):
         parcel_copy(i).wait_recv()
         rows = pl.ds(pl.multiple_of(i * CH, CH), CH)
-        one_hots(cv[rows], oh, mk)
         fields = [pbuf[f, rows] for f in range(6)]
         slot = (lax.broadcasted_iota(jnp.int32, (CH, 128), 0) + i * CH) * 128 + lax.broadcasted_iota(
             jnp.int32, (CH, 128), 1
@@ -181,21 +177,19 @@
         deposits = [evap] + [evap * fields[f] for f in range(2, 6)]
         for v in range(5):
             hi = deposits[v].astype(BF).astype(F32)
-            for half, piece in enumerate((hi, deposits[v] - hi)):
-                for j in range(CH):
-                    at = (half * CH + j) * 128
-                    w[v * 128 : (v + 1) * 128, at : at + 128] = mk[:, j * 128 : (j + 1) * 128] * rows16(
-                        piece[j : j + 1], 8
-                    )
-        width = CH * 128
-        acc[...] += lax.dot_general(w[:, :width], oh[...], NT, preferred_element_type=F32) + lax.dot_general(
-            w[:, width:], oh[...], NT, preferred_element_type=F32
-        )
+            low = (deposits[v] - hi) * LOW
+            for j in range(CH):
+                at = slice(j * 128, (j + 1) * 128)
+                hot = mk[i, :, at]
+                w[v * 128 : (v + 1) * 128, at] = hot * rows16(hi[j : j + 1], 8)
+                w8[v * 128 : (v + 1) * 128, at] = (hot * rows16(low[j : j + 1], 8)).astype(F8)
+        acc[:640] += lax.dot_general(w[...], oh[i], NT, preferred_element_type=F32)
+        acc[640:] += lax.dot_general(w8[...], oh8[i], NT, preferred_element_type=F32)
         return carry
 
     lax.fori_loop(0, steps, scatter, 0)
     for v in range(5):
-        turned = acc[v * 128 : (v + 1) * 128].T
+        turned = (acc[v * 128 : (v + 1) * 128] + acc[640 + v * 128 : 768 + v * 128] * (1.0 / LOW)).T
         for k in range(32):
             res[k * 5 + v] += turned[8 * k : 8 * k + 8]
 
@@ -249,7 +243,7 @@
             k = i if forward else 31 - i
             return plane(k, carry, rate, jac, first, final)
 
-        last = lax.fori_loop(0, 32, body, inflow)
+        last = lax.fori_loop(0, 32, body, inflow, unroll=4)
 
         @pl.when(a == sender)
         def _():
@@ -290,8 +284,8 @@
         out, left = pl.pallas_call(
             functools.partial(kernel, nsec),
             out_shape=(
-                jax.ShapeDtypeStruct((160, 8, 128), F32),
-                jax.ShapeDtypeStruct((256, 128), F32),
+                pltpu.VMEM((160, 8, 128), F32),
+                pltpu.VMEM((256, 128), F32),
             ),
             in_specs=[hbm, hbm, hbm, hbm, smem, smem, hbm, hbm, smem],
             out_specs=(vmem, vmem),
@@ -304,15 +298,17 @@
                 pltpu.VMEM((6, 256, 128), F32),
                 pltpu.VMEM((256, 128), F32),
                 pltpu.VMEM((256, 256), BF),
-                pltpu.VMEM((256, width), BF),
-                pltpu.VMEM((128, width), BF),
-                pltpu.VMEM((640, 2 * width), BF),
-                pltpu.VMEM((640, 256), F32),
+                pltpu.VMEM((steps, 256, width), BF),
+                pltpu.VMEM((steps, 256, width), F8),
+                pltpu.VMEM((steps, 128, width), BF),
+                pltpu.VMEM((640, width), BF),
+                pltpu.VMEM((640, width), F8),
+                pltpu.VMEM((1280, 256), F32),
                 pltpu.VMEM((160, 8, 128), F32),
                 pltpu.VMEM((160, 8, 128), F32),
                 pltpu.VMEM((160, 8, 128), F32),
-                pltpu.VMEM((32, 8, 128), F32),
-                pltpu.VMEM((32, 8, 128), F32),
+                pltpu.VMEM((160, 128), F32),
+                pltpu.VMEM((160, 128), F32),
                 pltpu.VMEM((16, 128), F32),
                 pltpu.VMEM((16, 128), F32),
                 pltpu.VMEM((16, 128), F32),

time: 69.4 us -> 53.4 us (0.77)
  Pallas kernels: 64.3 us -> 50.5 us
  local copies, waits for them, and re-layouts: 3.53 us -> 1.49 us
    pallas_call x1, Pallas kernels: 64.3 us -> 50.5 us  [local(): pl.pallas_call(functools.partial(kernel, nsec), out_shape=(pltpu.VMEM((16...]
    unnamed x2, local copies, waits for them, and re-layouts: 3.53 us -> 1.49 us
where the time goes in v1:
time: 53.4 us; the launch traced here: 53.3 us
  Pallas kernels  50.5 us (95%)
  local copies, waits for them, and re-layouts  1.49 us (3%)
  between operations  1.29 us (2%)
    pallas_call x1, Pallas kernels, local(): pl.pallas_call(functools.partial(kernel, nsec), out_shape=(pltpu.VMEM((16...  50.5 us
    unnamed x2, local copies, waits for them, and re-layouts  1.49 us

profile of v1, /device:TPU:1, one launch (start us, length us, event | category | flops | bytes accessed | tf_op | source)
XLA Modules:
  0.0 53.3 jit_solution(16815478784290136028)
XLA Ops:
  1.3 50.5 %shard_map.104 = (f32[160,8,128]{2,1,0:T(8,128)S(1)}, f32[256,128]{1,0:T(8,128)S(1)}) custom-call(f32[160,8,128]{2,1,0:T(8,128)} %bitcast.12, f32[800,8,128]{2,1,0:T(8,128)} %bitcast.10, f32[32,8,128]{2,1,0:T(8,128)} %lrate.1, f32[32,8,128]{2,1,0:T(8,128)} %urate.1, f32[5,5]{1,0:T(8,128)} %ljac.1, f32[5,5]{1,0:T(8,128)} %ujac.1, f32[6,256,128]{2,1,0:T(8,128)} %bitcast.11, ...), custom_call_target="tpu_custom_call" | custom-call | tf_op jit(solution)/shard_map/pallas_call | solution.py:284
  51.8 0.8 %copy.13 = f32[32,5,8,128]{3,2,1,0:T(8,128)} copy(f32[32,5,8,128]{3,2,1,0:T(8,128)S(1)} %bitcast.8) | data formatting | bytes 1310720
  52.6 0.7 %copy.14 = f32[1,1,32768]{2,1,0:T(1,128)} copy(f32[1,1,32768]{2,1,0:T(1,128)S(1)} %bitcast.9) | data formatting | bytes 262144

commit v2 on v1

--- a/solution.py
+++ b/solution.py
@@ -15,6 +15,7 @@
 DIFFUSE = 0.15
 SWIRL = 0.6
 CH = 32
+EARLY = 4
 LOW = 8192.0
 
 
@@ -25,19 +26,6 @@
 def rows16(row, times):
     packed = jnp.broadcast_to(row, (16, 128)).astype(BF)
     return jnp.concatenate([packed] * times, axis=0)
-
-
-def one_hots(cells, i, oh, oh8, mk):
-    row = lax.shift_right_logical(cells, 7).astype(F32)
-    lane = (cells & 127).astype(F32)
-    index = lax.broadcasted_iota(jnp.int32, (256, 128), 0).astype(F32).astype(BF)
-    one, zero = jnp.ones((), BF), jnp.zeros((), BF)
-    for j in range(CH):
-        at = slice(j * 128, (j + 1) * 128)
-        hot = jnp.where(index == rows16(row[j : j + 1], 16), one, zero)
-        oh[i, :, at] = hot
-        oh8[i, :, at] = hot.astype(F8)
-        mk[i, :, at] = jnp.where(index[:128] == rows16(lane[j : j + 1], 8), one, zero)
 
 
 def kernel(
@@ -89,6 +77,35 @@
         hi = turned.astype(BF)
         g2[0:128, h * 128 : (h + 1) * 128] = hi
         g2[128:256, h * 128 : (h + 1) * 128] = (turned - hi.astype(F32)).astype(BF)
+    local[1].wait()
+
+    index = lax.broadcasted_iota(jnp.int32, (256, 128), 0).astype(F32)
+    index = index.astype(BF)
+    one, zero = jnp.ones((), BF), jnp.zeros((), BF)
+
+    def gather(i, carry):
+        cells = cv[pl.ds(pl.multiple_of(i * CH, CH), CH)]
+        row = lax.shift_right_logical(cells, 7).astype(F32)
+        lane = (cells & 127).astype(F32)
+        table = g2[...]
+        for b in range(CH // 2):
+            hots = []
+            for j in (2 * b, 2 * b + 1):
+                at = slice(j * 128, (j + 1) * 128)
+                hot = jnp.where(index == rows16(row[j : j + 1], 16), one, zero)
+                oh[i, :, at] = hot
+                oh8[i, :, at] = hot.astype(F8)
+                mk[i, :, at] = jnp.where(index[:128] == rows16(lane[j : j + 1], 8), one, zero)
+                hots.append(hot)
+            found = jnp.dot(table, jnp.concatenate(hots, axis=1), preferred_element_type=F32)
+            picked = (found[:128] + found[128:]) * mk[i, :, b * 256 : (b + 1) * 256].astype(F32)
+            total = jnp.sum(jnp.sum(picked.reshape(16, 8, 256), axis=0), axis=0, keepdims=True)
+            for j in range(2):
+                gas[pl.ds(i * CH + 2 * b + j, 1), :] = total[:, j * 128 : (j + 1) * 128]
+        return carry
+
+    early = jnp.where(s == 0, EARLY, 0)
+    lax.fori_loop(0, early, gather, 0)
     pl.semaphore_wait(barrier, 4)
     halo = [
         remote(state.at[pl.ds(155 * (1 - a), 5)], sx.at[pl.ds(165 * a, 5)], hsend.at[0], hrecv.at[0], (s, 1 - a, r)),
@@ -96,7 +113,7 @@
         remote(upsend, uprecv, hsend.at[2], hrecv.at[2], (nxt, a, r)),
         remote(dnsend, dnrecv, hsend.at[3], hrecv.at[3], (prv, a, r)),
     ]
-    for copy in halo:
+    for copy in (halo[0], halo[2], halo[3]):
         copy.start()
 
     def send_parcels(c, carry):
@@ -104,20 +121,10 @@
         return carry
 
     lax.fori_loop(0, steps, send_parcels, 0)
-
-    local[1].wait()
-
-    def gather(i, carry):
-        rows = pl.ds(pl.multiple_of(i * CH, CH), CH)
-        one_hots(cv[rows], i, oh, oh8, mk)
-        found = jnp.dot(g2[...], oh[i], preferred_element_type=F32)
-        picked = (found[:128] + found[128:]) * mk[i].astype(F32)
-        total = jnp.sum(jnp.sum(picked.reshape(16, 8, CH * 128), axis=0), axis=0, keepdims=True)
-        for j in range(CH):
-            gas[pl.ds(i * CH + j, 1), :] = total[:, j * 128 : (j + 1) * 128]
-        return carry
-
-    lax.fori_loop(0, steps, gather, 0)
+    halo[1].start()
+
+
+    lax.fori_loop(early, steps, gather, 0)
 
     @pl.when(a == 0)
     def _():
@@ -127,7 +134,7 @@
     def _():
         sx[165:170] = jnp.zeros((5, 8, 128), F32)
 
-    for copy in halo:
+    for copy in (halo[0], halo[2], halo[3]):
         copy.wait_recv()
     sub = lax.broadcasted_iota(jnp.int32, (128, 128), 0)
     for q in range(10):
@@ -141,14 +148,12 @@
     lane8 = lax.broadcasted_iota(jnp.int32, (8, 128), 1)
     seam = sub8 == 7 * (1 - r)
 
-    def flux(k, carry):
+    def flux(k):
         for u in range(5):
             i = k * 5 + u
             x = sx[5 + i]
-            radial = (
-                jnp.where(sub8 == 0, 0.0, pltpu.roll(x, 1, 0))
-                + jnp.where(sub8 == 7, 0.0, pltpu.roll(x, 7, 0))
-                + jnp.where(seam, jnp.broadcast_to(rrecv[pl.ds(i, 1)], (8, 128)), 0.0)
+            radial = jnp.where(sub8 == 0, 0.0, pltpu.roll(x, 1, 0)) + jnp.where(
+                sub8 == 7, 0.0, pltpu.roll(x, 7, 0)
             )
             below = jnp.where(lane8 == 0, 0.0, pltpu.roll(x, 1, 1))
             above = jnp.where(lane8 == 127, 0.0, pltpu.roll(x, 127, 1))
@@ -156,9 +161,7 @@
             res[i] = (
                 DIFFUSE * beside + (DIFFUSE + SWIRL) * below + edge[i] - (6.0 * DIFFUSE + SWIRL) * x
             )
-        return carry
-
-    lax.fori_loop(0, 32, flux, 0, unroll=4)
+
 
     acc[...] = jnp.zeros_like(acc)
     live_count = count[0]
@@ -183,15 +186,20 @@
                 hot = mk[i, :, at]
                 w[v * 128 : (v + 1) * 128, at] = hot * rows16(hi[j : j + 1], 8)
                 w8[v * 128 : (v + 1) * 128, at] = (hot * rows16(low[j : j + 1], 8)).astype(F8)
+        for k in range(32 // steps):
+            flux(i * (32 // steps) + k)
         acc[:640] += lax.dot_general(w[...], oh[i], NT, preferred_element_type=F32)
         acc[640:] += lax.dot_general(w8[...], oh8[i], NT, preferred_element_type=F32)
         return carry
 
     lax.fori_loop(0, steps, scatter, 0)
+    halo[1].wait_recv()
     for v in range(5):
         turned = (acc[v * 128 : (v + 1) * 128] + acc[640 + v * 128 : 768 + v * 128] * (1.0 / LOW)).T
         for k in range(32):
-            res[k * 5 + v] += turned[8 * k : 8 * k + 8]
+            i = k * 5 + v
+            ring = jnp.where(seam, jnp.broadcast_to(DIFFUSE * rrecv[i : i + 1], (8, 128)), 0.0)
+            res[i] += turned[8 * k : 8 * k + 8] + ring
 
     for copy in local[2:]:
         copy.wait()

time: 53.4 us -> 47.7 us (0.89)
  Pallas kernels: 50.5 us -> 44.8 us
    pallas_call x1, Pallas kernels: 50.5 us -> 44.8 us  [local(): pl.pallas_call(functools.partial(kernel, nsec), out_shape=(pltpu.VMEM((16...]
where the time goes in v2:
time: 47.7 us; the launch traced here: 47.6 us
  Pallas kernels  44.8 us (94%)
  local copies, waits for them, and re-layouts  1.49 us (3%)
  between operations  1.29 us (3%)
    pallas_call x1, Pallas kernels, local(): pl.pallas_call(functools.partial(kernel, nsec), out_shape=(pltpu.VMEM((16...  44.8 us
    unnamed x2, local copies, waits for them, and re-layouts  1.49 us

profile of v2, /device:TPU:1, one launch (start us, length us, event | category | flops | bytes accessed | tf_op | source)
XLA Modules:
  0.0 47.6 jit_solution(5736700527274412630)
XLA Ops:
  1.3 44.8 %shard_map.104 = (f32[160,8,128]{2,1,0:T(8,128)S(1)}, f32[256,128]{1,0:T(8,128)S(1)}) custom-call(f32[160,8,128]{2,1,0:T(8,128)} %bitcast.12, f32[800,8,128]{2,1,0:T(8,128)} %bitcast.10, f32[32,8,128]{2,1,0:T(8,128)} %lrate.1, f32[32,8,128]{2,1,0:T(8,128)} %urate.1, f32[5,5]{1,0:T(8,128)} %ljac.1, f32[5,5]{1,0:T(8,128)} %ujac.1, f32[6,256,128]{2,1,0:T(8,128)} %bitcast.11, ...), custom_call_target="tpu_custom_call" | custom-call | tf_op jit(solution)/shard_map/pallas_call | solution.py:292
  46.1 0.8 %copy.13 = f32[32,5,8,128]{3,2,1,0:T(8,128)} copy(f32[32,5,8,128]{3,2,1,0:T(8,128)S(1)} %bitcast.8) | data formatting | bytes 1310720
  46.9 0.7 %copy.14 = f32[1,1,32768]{2,1,0:T(1,128)} copy(f32[1,1,32768]{2,1,0:T(1,128)S(1)} %bitcast.9) | data formatting | bytes 262144

commit v3 on v2

--- a/solution.py
+++ b/solution.py
@@ -32,7 +32,7 @@
     nsec,
     state, binv, lrate, urate, ljac, ujac, parcels, cell, count,
     out, left,
-    sx, bv, lv, uv, cv, pbuf, gas, g2, oh, oh8, mk, w, w8, acc, res, tgt, edge,
+    sx, bv, lv, uv, cv, pbuf, gas, g2, oh, oh8, mk, w, w8, acc, res, tgt, phi, xs, edge,
     rsend, rrecv, upsend, uprecv, dnsend, dnrecv, face, fsend,
     lsem, psend, precv, hsend, hrecv, rlsend, rlrecv,
 ):
@@ -104,6 +104,34 @@
                 gas[pl.ds(i * CH + 2 * b + j, 1), :] = total[:, j * 128 : (j + 1) * 128]
         return carry
 
+    mix = [[jnp.where(a == 1, ljac[u, v], ujac[u, v]) for v in range(5)] for u in range(5)]
+    for u in range(5):
+        for v in range(5):
+            phi[u * 5 + v] = jnp.full((8, 128), 1.0 if u == v else 0.0, F32)
+
+    def influence(i):
+        k = jnp.where(a == 1, i, 31 - i)
+        rate = jnp.where(a == 1, lv[k], uv[k])
+        for c in range(5):
+            column = [phi[v * 5 + c] for v in range(5)]
+            push = [rate * sum5([mix[u][v] * column[v] for v in range(5)]) for u in range(5)]
+            for u in range(5):
+                xs[k * 25 + u * 5 + c] = push[u]
+                phi[u * 5 + c] = -sum5([bv[k * 25 + u * 5 + v] * push[v] for v in range(5)])
+
+    def influence_planes(i, carry):
+        for k in range(4):
+            influence(i * 4 + k)
+        return carry
+
+    waits = lax.rem(s, 8) == 0
+
+    @pl.when(waits)
+    def _():
+        for copy in local[2:]:
+            copy.wait()
+        lax.fori_loop(0, 8, influence_planes, 0)
+
     early = jnp.where(s == 0, EARLY, 0)
     lax.fori_loop(0, early, gather, 0)
     pl.semaphore_wait(barrier, 4)
@@ -123,6 +151,12 @@
     lax.fori_loop(0, steps, send_parcels, 0)
     halo[1].start()
 
+
+    @pl.when(jnp.logical_not(waits))
+    def _():
+        for copy in local[2:]:
+            copy.wait()
+        lax.fori_loop(0, 8, influence_planes, 0)
 
     lax.fori_loop(early, steps, gather, 0)
 
@@ -178,14 +212,14 @@
         evap = mass * frac
         left[rows] = mass * (1.0 - frac)
         deposits = [evap] + [evap * fields[f] for f in range(2, 6)]
-        for v in range(5):
-            hi = deposits[v].astype(BF).astype(F32)
-            low = (deposits[v] - hi) * LOW
-            for j in range(CH):
-                at = slice(j * 128, (j + 1) * 128)
-                hot = mk[i, :, at]
-                w[v * 128 : (v + 1) * 128, at] = hot * rows16(hi[j : j + 1], 8)
-                w8[v * 128 : (v + 1) * 128, at] = (hot * rows16(low[j : j + 1], 8)).astype(F8)
+        his = [deposit.astype(BF).astype(F32) for deposit in deposits]
+        lows = [(deposit - hi) * LOW for deposit, hi in zip(deposits, his)]
+        for j in range(CH):
+            at = slice(j * 128, (j + 1) * 128)
+            hot = mk[i, :, at]
+            for v in range(5):
+                w[v * 128 : (v + 1) * 128, at] = hot * rows16(his[v][j : j + 1], 8)
+                w8[v * 128 : (v + 1) * 128, at] = (hot * rows16(lows[v][j : j + 1], 8)).astype(F8)
         for k in range(32 // steps):
             flux(i * (32 // steps) + k)
         acc[:640] += lax.dot_general(w[...], oh[i], NT, preferred_element_type=F32)
@@ -201,14 +235,12 @@
             ring = jnp.where(seam, jnp.broadcast_to(DIFFUSE * rrecv[i : i + 1], (8, 128)), 0.0)
             res[i] += turned[8 * k : 8 * k + 8] + ring
 
-    for copy in local[2:]:
-        copy.wait()
     zeros = tuple(jnp.zeros((8, 128), F32) for _ in range(5))
 
     def product(jac, values):
         return [sum5([jac[u, v] * values[v] for v in range(5)]) for u in range(5)]
 
-    def plane(k, carry, rate, jac, first, final):
+    def plane(k, carry, face, rate, jac, first, final):
         pushed = product(jac, carry)
         base = k * 5
         rk = rate[k]
@@ -220,7 +252,7 @@
                 d = r_u - term
                 tgt[base + u] = d
             else:
-                d = tgt[base + u] - term
+                d = (tgt[base + u] - sum5([xs[(base + u) * 5 + c] * face[c] for c in range(5)])) - term
                 if not final:
                     tgt[base + u] = r_u - term
             net.append(d)
@@ -235,21 +267,32 @@
 
     def half_sweep(hop, forward, first, final):
         sender = 0 if forward else 1
-
-        @pl.when(a == 1 - sender)
-        def _():
-            relay(hop).wait_recv()
-
-        @pl.when(a == sender)
-        def _():
-            face[hop] = jnp.zeros((5, 8, 128), F32)
-
-        inflow = tuple(face[hop, u] for u in range(5))
+        if not first:
+            @pl.when(a == sender)
+            def _():
+                relay(hop - 1).wait_recv()
+
+            @pl.when(a == 1 - sender)
+            def _():
+                face[hop - 1] = jnp.zeros((5, 8, 128), F32)
+        if final:
+            @pl.when(a == 1 - sender)
+            def _():
+                relay(hop).wait_recv()
+
+            @pl.when(a == sender)
+            def _():
+                face[hop] = jnp.zeros((5, 8, 128), F32)
+
+            inflow = tuple(face[hop, u] for u in range(5))
+        else:
+            inflow = zeros
+        past = None if first else tuple(face[hop - 1, u] for u in range(5))
         rate, jac = (lv, ljac) if forward else (uv, ujac)
 
         def body(i, carry):
             k = i if forward else 31 - i
-            return plane(k, carry, rate, jac, first, final)
+            return plane(k, carry, past, rate, jac, first, final)
 
         last = lax.fori_loop(0, 32, body, inflow, unroll=4)
 
@@ -314,6 +357,8 @@
                 pltpu.VMEM((1280, 256), F32),
                 pltpu.VMEM((160, 8, 128), F32),
                 pltpu.VMEM((160, 8, 128), F32),
+                pltpu.VMEM((25, 8, 128), F32),
+                pltpu.VMEM((800, 8, 128), F32),
                 pltpu.VMEM((160, 8, 128), F32),
                 pltpu.VMEM((160, 128), F32),
                 pltpu.VMEM((160, 128), F32),

time: 47.7 us -> 46.7 us (0.979)
  Pallas kernels: 44.8 us -> 43.8 us
    pallas_call x1, Pallas kernels: 44.8 us -> 43.8 us  [local(): pl.pallas_call(functools.partial(kernel, nsec), out_shape=(pltpu.VMEM((16...]
where the time goes in v3:
time: 46.7 us; the launch traced here: 46.6 us
  Pallas kernels  43.8 us (94%)
  local copies, waits for them, and re-layouts  1.49 us (3%)
  between operations  1.29 us (3%)
    pallas_call x1, Pallas kernels, local(): pl.pallas_call(functools.partial(kernel, nsec), out_shape=(pltpu.VMEM((16...  43.8 us
    unnamed x2, local copies, waits for them, and re-layouts  1.49 us

profile of v3, /device:TPU:1, one launch (start us, length us, event | category | flops | bytes accessed | tf_op | source)
XLA Modules:
  0.0 46.6 jit_solution(13270641131149122325)
XLA Ops:
  1.3 43.8 %shard_map.104 = (f32[160,8,128]{2,1,0:T(8,128)S(1)}, f32[256,128]{1,0:T(8,128)S(1)}) custom-call(f32[160,8,128]{2,1,0:T(8,128)} %bitcast.12, f32[800,8,128]{2,1,0:T(8,128)} %bitcast.10, f32[32,8,128]{2,1,0:T(8,128)} %lrate.1, f32[32,8,128]{2,1,0:T(8,128)} %urate.1, f32[5,5]{1,0:T(8,128)} %ljac.1, f32[5,5]{1,0:T(8,128)} %ujac.1, f32[6,256,128]{2,1,0:T(8,128)} %bitcast.11, ...), custom_call_target="tpu_custom_call" | custom-call | tf_op jit(solution)/shard_map/pallas_call | solution.py:335
  45.1 0.8 %copy.13 = f32[32,5,8,128]{3,2,1,0:T(8,128)} copy(f32[32,5,8,128]{3,2,1,0:T(8,128)S(1)} %bitcast.8) | data formatting | bytes 1310720
  45.9 0.7 %copy.14 = f32[1,1,32768]{2,1,0:T(1,128)} copy(f32[1,1,32768]{2,1,0:T(1,128)S(1)} %bitcast.9) | data formatting | bytes 262144

commit v4 on v3

--- a/solution.py
+++ b/solution.py
@@ -15,6 +15,7 @@
 DIFFUSE = 0.15
 SWIRL = 0.6
 CH = 32
+NEAR = 4
 EARLY = 4
 LOW = 8192.0
 
@@ -126,11 +127,10 @@
 
     waits = lax.rem(s, 8) == 0
 
-    @pl.when(waits)
-    def _():
-        for copy in local[2:]:
-            copy.wait()
-        lax.fori_loop(0, 8, influence_planes, 0)
+    for copy in local[2:]:
+        copy.wait()
+    ahead = jnp.where(waits, 8, jnp.where(lax.rem(s, 8) == 7, 0, NEAR))
+    lax.fori_loop(0, ahead, influence_planes, 0)
 
     early = jnp.where(s == 0, EARLY, 0)
     lax.fori_loop(0, early, gather, 0)
@@ -152,12 +152,7 @@
     halo[1].start()
 
 
-    @pl.when(jnp.logical_not(waits))
-    def _():
-        for copy in local[2:]:
-            copy.wait()
-        lax.fori_loop(0, 8, influence_planes, 0)
-
+    lax.fori_loop(ahead, 8, influence_planes, 0)
     lax.fori_loop(early, steps, gather, 0)
 
     @pl.when(a == 0)

time: 46.7 us -> 47.4 us (1.015)
  Pallas kernels: 43.8 us -> 44.5 us
    pallas_call x1, Pallas kernels: 43.8 us -> 44.5 us  [local(): pl.pallas_call(functools.partial(kernel, nsec), out_shape=(pltpu.VMEM((16...]
where the time goes in v4:
time: 47.4 us; the launch traced here: 47.3 us
  Pallas kernels  44.5 us (94%)
  local copies, waits for them, and re-layouts  1.49 us (3%)
  between operations  1.29 us (3%)
    pallas_call x1, Pallas kernels, local(): pl.pallas_call(functools.partial(kernel, nsec), out_shape=(pltpu.VMEM((16...  44.5 us
    unnamed x2, local copies, waits for them, and re-layouts  1.49 us

profile of v4, /device:TPU:1, one launch (start us, length us, event | category | flops | bytes accessed | tf_op | source)
XLA Modules:
  0.0 47.3 jit_solution(7477414249883880939)
XLA Ops:
  1.3 44.5 %shard_map.104 = (f32[160,8,128]{2,1,0:T(8,128)S(1)}, f32[256,128]{1,0:T(8,128)S(1)}) custom-call(f32[160,8,128]{2,1,0:T(8,128)} %bitcast.12, f32[800,8,128]{2,1,0:T(8,128)} %bitcast.10, f32[32,8,128]{2,1,0:T(8,128)} %lrate.1, f32[32,8,128]{2,1,0:T(8,128)} %urate.1, f32[5,5]{1,0:T(8,128)} %ljac.1, f32[5,5]{1,0:T(8,128)} %ujac.1, f32[6,256,128]{2,1,0:T(8,128)} %bitcast.11, ...), custom_call_target="tpu_custom_call" | custom-call | tf_op jit(solution)/shard_map/pallas_call | solution.py:330
  45.8 0.8 %copy.13 = f32[32,5,8,128]{3,2,1,0:T(8,128)} copy(f32[32,5,8,128]{3,2,1,0:T(8,128)S(1)} %bitcast.8) | data formatting | bytes 1310720
  46.6 0.7 %copy.14 = f32[1,1,32768]{2,1,0:T(1,128)} copy(f32[1,1,32768]{2,1,0:T(1,128)S(1)} %bitcast.9) | data formatting | bytes 262144
